TPU v7x, 32 devices: a whole 2x2x4 slice. The times are simulated.
32 devices in a mesh: pipe: 4 (over y, core), ctx: 8 (over z, x).
Axes of the slice: x: 2, y: 2, z: 4, core: 2. Of those that a mesh axis runs over, the one named last changes fastest.
Arguments:
- x_proj: bfloat16 [4, 2, 1024, 2048], P('pipe', None, 'ctx'), may hold values from -6 to 6
- gate_proj: bfloat16 [4, 2, 1024, 2048], P('pipe', None, 'ctx'), may hold values from -6 to 6
- bc_proj: bfloat16 [4, 2, 1024, 1024], P('pipe', None, 'ctx'), may hold values from -6 to 6
- dt_raw: float32 [4, 2, 1024, 64], P('pipe', None, 'ctx'), may hold values from -3 to 16
- decay_rate: float32 [4, 64], P('pipe'), may hold values from 0 to 1
- conv_weight: float32 [4, 4, 3072], P('pipe'), may hold values from -3 to 3
- skip_gain: float32 [4, 64], P('pipe'), may hold values from 0.5 to 1.5
- norm_gain: float32 [4, 2048], P('pipe'), may hold values from 0.1 to 1.9
Outputs:
- mixed_out: bfloat16 [4, 2, 1024, 2048], P('pipe', None, 'ctx')
All inputs are finite; a program needn't handle non-finite values.
Results may differ from a plain program's by a relative error of at most 0.0052.
Values may be sent and summed in bfloat16 or wider, within the bound.
A program may use at most 64 MiB of HBM per device.

v0:
```python
import jax
import jax.numpy as jnp
from jax import lax
from jax.sharding import PartitionSpec as P

HEADS = 64
HEAD_DIM = 32
GROUPS = 8
STATE = 64
BLOCK = 128
SEQS = 2


norm_eps = 1e-05


def from_behind(block, axis, distance):
    devices = range(lax.axis_size(axis))
    route = [(i - distance, i) for i in devices if i - distance in devices]
    return lax.ppermute(block, axis, route)


def carried_in(x, axis, combine, identity):
    count, mine = (lax.axis_size(axis), lax.axis_index(axis))
    everything = jax.tree.map(lambda part: lax.all_gather(part, axis), x)
    start = jax.tree.map(
        lambda part, zero: jnp.broadcast_to(jnp.asarray(zero, part.dtype), part.shape), x, identity
    )

    def turn(k, before):
        reached = k < mine
        new = combine(before, jax.tree.map(lambda part: part[k], everything))
        return jax.tree.map(lambda a, b: jnp.where(reached, a, b), new, before)

    return lax.fori_loop(0, count, turn, start)


def convolve(inputs, weight, head_rows):
    tap_count = weight.shape[0]
    padded = jnp.concatenate([head_rows, inputs], axis=0)
    length = inputs.shape[0]
    conv_sum = weight[0] * padded[0:length]
    for offset in range(1, tap_count):
        conv_sum = conv_sum + weight[offset] * padded[offset : offset + length]
    return jax.nn.silu(conv_sum).astype(jnp.bfloat16)


def block_terms(activated, dt_rows, rates):
    feature_width = HEADS * HEAD_DIM
    bc_width = GROUPS * STATE
    per_group = HEADS // GROUPS
    block_count = activated.shape[0] // BLOCK
    inputs_x = activated[:, :feature_width].reshape(block_count, BLOCK, HEADS, HEAD_DIM)
    inputs_b = activated[:, feature_width : feature_width + bc_width].reshape(
        block_count, BLOCK, GROUPS, STATE
    )
    inputs_c = activated[:, feature_width + bc_width :].reshape(block_count, BLOCK, GROUPS, STATE)
    steps_dt = jax.nn.softplus(dt_rows).reshape(block_count, BLOCK, HEADS)
    cumulated = jnp.cumsum(-steps_dt * rates, axis=1)
    scores = jnp.einsum("cign,cjgn->cgij", inputs_c, inputs_b, preferred_element_type=jnp.float32)
    scores = jnp.repeat(scores, per_group, axis=1)
    cumul_heads = jnp.transpose(cumulated, (0, 2, 1))
    lower_mask = jnp.arange(BLOCK)[:, None] >= jnp.arange(BLOCK)[None, :]
    log_gaps = cumul_heads[:, :, :, None] - cumul_heads[:, :, None, :]
    decays = jnp.where(lower_mask, jnp.exp(jnp.where(lower_mask, log_gaps, 0.0)), 0.0)
    dt_heads = jnp.transpose(steps_dt, (0, 2, 1))
    weights = (scores * decays * dt_heads[:, :, None, :]).astype(jnp.bfloat16)
    diag_out = jnp.einsum("chij,cjhp->cihp", weights, inputs_x, preferred_element_type=jnp.float32)
    block_ends = cumulated[:, -1, :]
    tail_weight = jnp.exp(block_ends[:, None, :] - cumulated) * steps_dt
    keyed_rows = (
        jnp.repeat(inputs_b, per_group, axis=2).astype(jnp.float32) * tail_weight[..., None]
    ).astype(jnp.bfloat16)
    local_states = jnp.einsum(
        "cqhn,cqhp->chpn", keyed_rows, inputs_x, preferred_element_type=jnp.float32
    )
    return (inputs_x, inputs_c, cumulated, diag_out, local_states, jnp.exp(block_ends))


def finish(inputs_x, inputs_c, cumulated, diag_out, incoming, skips, gate_rows, gains):
    per_group = HEADS // GROUPS
    state_rows = incoming.astype(jnp.bfloat16)
    off_out = jnp.einsum(
        "cqhn,chpn->cqhp",
        jnp.repeat(inputs_c, per_group, axis=2),
        state_rows,
        preferred_element_type=jnp.float32,
    )
    off_out = off_out * jnp.exp(cumulated)[..., None]
    mixed_sum = diag_out + off_out + skips[None, None, :, None] * inputs_x.astype(jnp.float32)
    length = mixed_sum.shape[0] * mixed_sum.shape[1]
    feature_width = HEADS * HEAD_DIM
    gated_rows = mixed_sum.reshape(length, feature_width) * jax.nn.silu(
        gate_rows.astype(jnp.float32)
    )
    grouped = gated_rows.reshape(length, GROUPS, feature_width // GROUPS)
    inv_rms = lax.rsqrt(jnp.mean(grouped * grouped, axis=-1, keepdims=True) + norm_eps)
    return ((grouped * inv_rms).reshape(length, feature_width) * gains).astype(jnp.bfloat16)


def walk_blocks(factors, local_states):

    def advance(step_pair_in, step_pair):
        held_state, held_decay = step_pair_in
        factor, own_term = step_pair
        following = (factor[:, None, None] * held_state + own_term, factor * held_decay)
        return (following, (held_state, held_decay))

    start_pair = (
        jnp.zeros(local_states.shape[1:], jnp.float32),
        jnp.ones(factors.shape[1:], jnp.float32),
    )
    totals, emitted = lax.scan(advance, start_pair, (factors, local_states))
    return (emitted[0], emitted[1], totals[0], totals[1])


def combine(earlier, latter):
    return (earlier[0] * latter[0], latter[0][..., None, None] * earlier[1] + latter[1])


def on_device(x_proj, gate_proj, bc_proj, dt_raw, decay_rate, conv_weight, skip_gain, norm_gain):
    section = lax.axis_index("pipe")
    sections = lax.axis_size("pipe")
    per_tick = 1
    rounds = SEQS // per_tick
    tick_count = rounds + sections - 1
    tok_rows = x_proj.shape[2]
    feature_width = x_proj.shape[3]
    rates = decay_rate[0]
    weight = conv_weight[0]
    skips = skip_gain[0]
    gains = norm_gain[0]
    tap_count = weight.shape[0]

    def one_tick(step, loop_state):
        previous, collected = loop_state
        slot_idx = step - section
        active = (slot_idx >= 0) & (slot_idx < rounds)
        row_start = jnp.clip(slot_idx, 0, rounds - 1) * per_tick
        x_rows = lax.dynamic_slice_in_dim(x_proj[0], row_start, per_tick, 0)
        bc_rows = lax.dynamic_slice_in_dim(bc_proj[0], row_start, per_tick, 0)
        dt_rows = lax.dynamic_slice_in_dim(dt_raw[0], row_start, per_tick, 0)
        gate_rows = lax.dynamic_slice_in_dim(gate_proj[0], row_start, per_tick, 0)
        conv_in = jnp.concatenate(
            [
                x_rows.astype(jnp.float32) + previous.astype(jnp.float32),
                bc_rows.astype(jnp.float32),
            ],
            axis=2,
        )
        edge_rows = from_behind(conv_in[:, tok_rows - (tap_count - 1) :, :], "ctx", 1)
        activated = jax.vmap(convolve, in_axes=(0, None, 0))(conv_in, weight, edge_rows)
        span_parts = jax.vmap(block_terms, in_axes=(0, 0, None))(activated, dt_rows, rates)
        inputs_x, inputs_c, cumulated, diag_out, local_states, factors = span_parts
        prefix, before, total_state, total_decay = jax.vmap(walk_blocks)(factors, local_states)
        entering_decay, entering_state = carried_in(
            (total_decay, total_state),
            "ctx",
            combine,
            (jnp.ones_like(total_decay), jnp.zeros_like(total_state)),
        )
        incoming = before[:, :, :, None, None] * entering_state[:, None] + prefix
        layer_out = jax.vmap(finish, in_axes=(0, 0, 0, 0, 0, None, 0, None))(
            inputs_x, inputs_c, cumulated, diag_out, incoming, skips, gate_rows, gains
        )
        updated = lax.dynamic_update_slice_in_dim(collected, layer_out, row_start, 0)
        collected = jnp.where(active, updated, collected)
        previous = from_behind(layer_out, "pipe", 1)
        return (previous, collected)

    start_prev = jnp.zeros((per_tick, tok_rows, feature_width), jnp.bfloat16)
    start_out = jnp.zeros((SEQS, tok_rows, feature_width), jnp.bfloat16)
    final_prev, collected = lax.fori_loop(0, tick_count, one_tick, (start_prev, start_out))
    return collected[None]


def solution(mesh):
    in_specs = (
        P("pipe", None, "ctx", None),
        P("pipe", None, "ctx", None),
        P("pipe", None, "ctx", None),
        P("pipe", None, "ctx", None),
        P("pipe", None),
        P("pipe", None, None),
        P("pipe", None),
        P("pipe", None),
    )
    out_specs = P("pipe", None, "ctx", None)
    return jax.shard_map(
        on_device, mesh=mesh, in_specs=in_specs, out_specs=out_specs, check_vma=False
    )
```

profile of v0, /device:TPU:31, one launch (start us, length us, event | category | flops | bytes accessed | tf_op | source)
XLA Modules:
  0.0 821.1 jit_solution(3975791752927495552)
XLA Ops:
  8.5 806.1 %while.59 = (s32[]{:T(128)}, bf16[1,128,2048]{1,2,0:T(8,128)(2,1)}, bf16[2,128,2048]{2,1,0:T(8,128)(2,1)}, f32[4,3072]{1,0:T(4,128)}, s32[]{:T(128)}, /*index=5*...) while((s32[]{:T(128)}, bf16[1,128,2048]{1,2,0:T(8,128)(2,1)}, ...), condition=%wide.region_6.7_spmd, body=%wide.region_0.6_spmd.sunk | while | flops 173248592 | bytes 98463896 | solution.py:173
  13.0 2.8 collective-permute-done
  23.9 12.5 %all-gather.4 = f32[8,1,1,64]{3,2,1,0:T(1,128)S(1)} all-gather(f32[1,1,1,64]{3,2,1,0:T(1,128)S(1)} %get-tuple-element.637), channel_id=2, replica_groups=mesh['pipe'=4,'ctx'=8] {'ctx'}, dimensions={0}, use_global_device_ids=true | all-gather | bytes 2304 | tf_op jit(solution)/shard_map/while/body/eval_jaxpr/all_gather | solution.py:25
  39.6 104.3 %all-gather.8.cloned.1.call-done = f32[512,32,64]{2,1,0:T(8,128)} async-done(((f32[64,32,64]{2,1,0:T(8,128)}), f32[512,32,64]{2,1,0:T(8,128)}) %all-gather.8.cloned.1.call-update) | async-done | bytes 4194320 | tf_op jit(solution)/shard_map/while/body/eval_jaxpr/all_gather | solution.py:25
  144.0 12.2 %while.60 = (s32[]{:T(128)}, f32[1,64,32,64]{3,2,1,0:T(8,128)S(1)}, s32[]{:T(128)}, f32[8,1,64]{2,1,0:T(1,128)S(1)}, f32[8,1,64,32,64]{4,3,2,1,0:T(8,128)}, /*index=5*/s32[]{:T(128)}, s32[]{:T(128)}) while((s32[]{:T(128)}, f32[1,64,32,64]{3,2,1,0:T(8,128)S(1)}, s32[]{:T(128)}, f32[8,1,64]{2,1,0:T(1,128)S(1)}, ...), condition=%wide.region_3.3_spmd.clone, body=%wide.region_2.2_spmd.clone.sunk | while | flops 524292 | bytes 1573737 | solution.py:35
  161.4 2.3 collective-permute-done.1
  168.2 2.8 collective-permute-done
  179.1 12.5 %all-gather.4 = f32[8,1,1,64]{3,2,1,0:T(1,128)S(1)} all-gather(f32[1,1,1,64]{3,2,1,0:T(1,128)S(1)} %get-tuple-element.637), channel_id=2, replica_groups=mesh['pipe'=4,'ctx'=8] {'ctx'}, dimensions={0}, use_global_device_ids=true | all-gather | bytes 2304 | tf_op jit(solution)/shard_map/while/body/eval_jaxpr/all_gather | solution.py:25
  194.9 111.8 %all-gather.8.cloned.1.call-done = f32[512,32,64]{2,1,0:T(8,128)} async-done(((f32[64,32,64]{2,1,0:T(8,128)}), f32[512,32,64]{2,1,0:T(8,128)}) %all-gather.8.cloned.1.call-update) | async-done | bytes 4194320 | tf_op jit(solution)/shard_map/while/body/eval_jaxpr/all_gather | solution.py:25
  306.7 12.2 %while.60 = (s32[]{:T(128)}, f32[1,64,32,64]{3,2,1,0:T(8,128)S(1)}, s32[]{:T(128)}, f32[8,1,64]{2,1,0:T(1,128)S(1)}, f32[8,1,64,32,64]{4,3,2,1,0:T(8,128)}, /*index=5*/s32[]{:T(128)}, s32[]{:T(128)}) while((s32[]{:T(128)}, f32[1,64,32,64]{3,2,1,0:T(8,128)S(1)}, s32[]{:T(128)}, f32[8,1,64]{2,1,0:T(1,128)S(1)}, ...), condition=%wide.region_3.3_spmd.clone, body=%wide.region_2.2_spmd.clone.sunk | while | flops 524292 | bytes 1573737 | solution.py:35
  324.1 2.3 collective-permute-done.1
  330.9 2.8 collective-permute-done
  341.8 12.5 %all-gather.4 = f32[8,1,1,64]{3,2,1,0:T(1,128)S(1)} all-gather(f32[1,1,1,64]{3,2,1,0:T(1,128)S(1)} %get-tuple-element.637), channel_id=2, replica_groups=mesh['pipe'=4,'ctx'=8] {'ctx'}, dimensions={0}, use_global_device_ids=true | all-gather | bytes 2304 | tf_op jit(solution)/shard_map/while/body/eval_jaxpr/all_gather | solution.py:25
  357.6 111.8 %all-gather.8.cloned.1.call-done = f32[512,32,64]{2,1,0:T(8,128)} async-done(((f32[64,32,64]{2,1,0:T(8,128)}), f32[512,32,64]{2,1,0:T(8,128)}) %all-gather.8.cloned.1.call-update) | async-done | bytes 4194320 | tf_op jit(solution)/shard_map/while/body/eval_jaxpr/all_gather | solution.py:25
  469.4 12.2 %while.60 = (s32[]{:T(128)}, f32[1,64,32,64]{3,2,1,0:T(8,128)S(1)}, s32[]{:T(128)}, f32[8,1,64]{2,1,0:T(1,128)S(1)}, f32[8,1,64,32,64]{4,3,2,1,0:T(8,128)}, /*index=5*/s32[]{:T(128)}, s32[]{:T(128)}) while((s32[]{:T(128)}, f32[1,64,32,64]{3,2,1,0:T(8,128)S(1)}, s32[]{:T(128)}, f32[8,1,64]{2,1,0:T(1,128)S(1)}, ...), condition=%wide.region_3.3_spmd.clone, body=%wide.region_2.2_spmd.clone.sunk | while | flops 524292 | bytes 1573737 | solution.py:35
  493.6 2.8 collective-permute-done
  504.5 12.5 %all-gather.4 = f32[8,1,1,64]{3,2,1,0:T(1,128)S(1)} all-gather(f32[1,1,1,64]{3,2,1,0:T(1,128)S(1)} %get-tuple-element.637), channel_id=2, replica_groups=mesh['pipe'=4,'ctx'=8] {'ctx'}, dimensions={0}, use_global_device_ids=true | all-gather | bytes 2304 | tf_op jit(solution)/shard_map/while/body/eval_jaxpr/all_gather | solution.py:25
  520.3 111.8 %all-gather.8.cloned.1.call-done = f32[512,32,64]{2,1,0:T(8,128)} async-done(((f32[64,32,64]{2,1,0:T(8,128)}), f32[512,32,64]{2,1,0:T(8,128)}) %all-gather.8.cloned.1.call-update) | async-done | bytes 4194320 | tf_op jit(solution)/shard_map/while/body/eval_jaxpr/all_gather | solution.py:25
  632.1 12.2 %while.60 = (s32[]{:T(128)}, f32[1,64,32,64]{3,2,1,0:T(8,128)S(1)}, s32[]{:T(128)}, f32[8,1,64]{2,1,0:T(1,128)S(1)}, f32[8,1,64,32,64]{4,3,2,1,0:T(8,128)}, /*index=5*/s32[]{:T(128)}, s32[]{:T(128)}) while((s32[]{:T(128)}, f32[1,64,32,64]{3,2,1,0:T(8,128)S(1)}, s32[]{:T(128)}, f32[8,1,64]{2,1,0:T(1,128)S(1)}, ...), condition=%wide.region_3.3_spmd.clone, body=%wide.region_2.2_spmd.clone.sunk | while | flops 524292 | bytes 1573737 | solution.py:35
  649.5 2.3 collective-permute-done.1
  656.4 2.8 collective-permute-done
  667.2 12.5 %all-gather.4 = f32[8,1,1,64]{3,2,1,0:T(1,128)S(1)} all-gather(f32[1,1,1,64]{3,2,1,0:T(1,128)S(1)} %get-tuple-element.637), channel_id=2, replica_groups=mesh['pipe'=4,'ctx'=8] {'ctx'}, dimensions={0}, use_global_device_ids=true | all-gather | bytes 2304 | tf_op jit(solution)/shard_map/while/body/eval_jaxpr/all_gather | solution.py:25
  683.0 111.8 %all-gather.8.cloned.1.call-done = f32[512,32,64]{2,1,0:T(8,128)} async-done(((f32[64,32,64]{2,1,0:T(8,128)}), f32[512,32,64]{2,1,0:T(8,128)}) %all-gather.8.cloned.1.call-update) | async-done | bytes 4194320 | tf_op jit(solution)/shard_map/while/body/eval_jaxpr/all_gather | solution.py:25
  794.8 12.2 %while.60 = (s32[]{:T(128)}, f32[1,64,32,64]{3,2,1,0:T(8,128)S(1)}, s32[]{:T(128)}, f32[8,1,64]{2,1,0:T(1,128)S(1)}, f32[8,1,64,32,64]{4,3,2,1,0:T(8,128)}, /*index=5*/s32[]{:T(128)}, s32[]{:T(128)}) while((s32[]{:T(128)}, f32[1,64,32,64]{3,2,1,0:T(8,128)S(1)}, s32[]{:T(128)}, f32[8,1,64]{2,1,0:T(1,128)S(1)}, ...), condition=%wide.region_3.3_spmd.clone, body=%wide.region_2.2_spmd.clone.sunk | while | flops 524292 | bytes 1573737 | solution.py:35
  (459 shorter events, 169.6 us)
Async XLA Ops:
  8.5 2.4 copy-start.7
  8.5 135.5 %all-gather.8.cloned.1.call-start = ((), (), s32[]{:S(2)}) async-start(), calls=%async_computation | async-start | bytes 9437184 | tf_op jit(solution)/shard_map/while/body/eval_jaxpr/all_gather | solution.py:25
  11.1 4.7 collective-permute-start
  159.8 3.9 collective-permute-start.1
  161.4 2.4 copy-start.6
  163.7 2.4 copy-start.7
  163.7 142.9 %all-gather.8.cloned.1.call-start = ((), (), s32[]{:S(2)}) async-start(), calls=%async_computation | async-start | bytes 9437184 | tf_op jit(solution)/shard_map/while/body/eval_jaxpr/all_gather | solution.py:25
  166.4 4.7 collective-permute-start
  322.5 3.9 collective-permute-start.1
  324.1 2.4 copy-start.6
  326.5 2.4 copy-start.7
  326.5 142.9 %all-gather.8.cloned.1.call-start = ((), (), s32[]{:S(2)}) async-start(), calls=%async_computation | async-start | bytes 9437184 | tf_op jit(solution)/shard_map/while/body/eval_jaxpr/all_gather | solution.py:25
  329.1 4.7 collective-permute-start
  485.2 3.9 collective-permute-start.1
  486.8 2.4 copy-start.6
  489.2 2.4 copy-start.7
  489.2 142.9 %all-gather.8.cloned.1.call-start = ((), (), s32[]{:S(2)}) async-start(), calls=%async_computation | async-start | bytes 9437184 | tf_op jit(solution)/shard_map/while/body/eval_jaxpr/all_gather | solution.py:25
  491.8 4.7 collective-permute-start
  647.9 3.9 collective-permute-start.1
  651.9 2.4 copy-start.7
  651.9 142.9 %all-gather.8.cloned.1.call-start = ((), (), s32[]{:S(2)}) async-start(), calls=%async_computation | async-start | bytes 9437184 | tf_op jit(solution)/shard_map/while/body/eval_jaxpr/all_gather | solution.py:25
  654.5 4.7 collective-permute-start
  810.6 3.9 collective-permute-start.1
  812.2 2.4 copy-start.6
  (56 other events, 86.2 us)
Sparse Core Ops, SparseCore 0:
  19.6 124.3 all-gather.7
  174.8 131.8 all-gather.7
  337.5 131.8 all-gather.7
  500.2 131.8 all-gather.7
  662.9 131.8 all-gather.7
where the time goes:
time: 834 us; the launch traced here: 821 us
  waiting for transfers between devices  578 us (69%)
  other arithmetic  83.7 us (10%)
  blocking collectives  62.3 us (7%)
  local copies, waits for them, and re-layouts  50.1 us (6%)
  matrix products  18.1 us (2%)
  between operations  13.1 us (2%)
  starting transfers between devices  12.9 us (2%)
    all_gather x5, waiting for transfers between devices, carried_in(): everything = jax.tree.map(lambda part: lax.all_gather(part, axis), x)  552 us
    all_gather x5, blocking collectives, carried_in(): everything = jax.tree.map(lambda part: lax.all_gather(part, axis), x)  62.3 us
    select_n x40, other arithmetic, turn(): return jax.tree.map(lambda a, b: jnp.where(reached, a, b), new, before)  59.3 us
    ppermute x10, waiting for transfers between devices, from_behind(): return lax.ppermute(block, axis, route)  25.8 us
  transfers between devices with their start and end apart: 15, of which 15 were waited for; matrix products, arithmetic and copies ran while one was open for 5% of the time, Pallas kernels for 0%

commit v1 on v0

v1 whole, which is shorter than its diff:
```python
import functools

import jax
import jax.numpy as jnp
from jax import lax
from jax.experimental import pallas as pl
from jax.experimental.pallas import tpu as pltpu
from jax.sharding import PartitionSpec as P

HEADS = 64
HEAD_DIM = 32
GROUPS = 8
STATE = 64
BLOCK = 128
SEQS = 2
PER_GROUP = HEADS // GROUPS
WIDTH = PER_GROUP * HEAD_DIM
HD = HEADS * HEAD_DIM
UNITS = SEQS * GROUPS
EDGE = 16
TAPS = 4

norm_eps = 1e-05
MESH = pl.DeviceIdType.MESH
HIGHEST = lax.Precision.HIGHEST
STATE_DT = jnp.float32


def silu(v):
    half = 0.5 * v
    return half * jnp.tanh(half) + half


def conv(buf, weight):
    first = EDGE - TAPS + 1
    total = weight[0:1] * buf[first : first + BLOCK]
    for tap in range(1, TAPS):
        total = total + weight[tap : tap + 1] * buf[first + tap : first + tap + BLOCK]
    return silu(total)


def kernel(
    sections,
    ranges,
    x_ref,
    gate_ref,
    bc_ref,
    dt_ref,
    rate_ref,
    w_ref,
    skip_ref,
    gain_ref,
    out_ref,
    weights,
    b_rows,
    c_rows,
    ecum,
    tails,
    cum_cols,
    cum_t,
    dt_t,
    skips,
    cbuf,
    bbuf,
    x_head,
    bc_head,
    prev,
    edge,
    state_in,
    state_out,
    made,
    head_send,
    head_recv,
    prev_send,
    prev_recv,
    edge_send,
    edge_recv,
    state_send,
    state_recv,
):
    f32, bf16 = jnp.float32, jnp.bfloat16
    section = lax.axis_index("pipe")
    mine = lax.axis_index("ctx")
    has_next = section < sections - 1
    has_prev = section > 0
    has_right = mine < ranges - 1
    has_left = mine > 0

    barrier = pltpu.get_barrier_semaphore()
    partners = (
        (has_next, 1, 0),
        (has_next & has_right, 1, 1),
        (has_right, 0, 1),
        (has_prev, -1, 0),
        (has_prev & has_left, -1, -1),
        (has_left, 0, -1),
    )
    count = 0
    for there, down, along in partners:
        count = count + there.astype(jnp.int32)

        @pl.when(there)
        def _(down=down, along=along):
            pl.semaphore_signal(
                barrier,
                inc=1,
                device_id={"pipe": section + down, "ctx": mine + along},
                device_id_type=MESH,
            )

    def head_copy(src, dst, slot):
        return pltpu.make_async_remote_copy(
            src_ref=src.at[0, :, pl.ds(BLOCK - EDGE, EDGE), :],
            dst_ref=dst,
            send_sem=head_send.at[slot],
            recv_sem=head_recv.at[slot],
            device_id={"pipe": section, "ctx": mine + 1},
            device_id_type=MESH,
        )

    def prev_copy(u):
        return pltpu.make_async_remote_copy(
            src_ref=made.at[u],
            dst_ref=prev.at[u],
            send_sem=prev_send.at[u],
            recv_sem=prev_recv.at[u],
            device_id={"pipe": section + 1, "ctx": mine},
            device_id_type=MESH,
        )

    def edge_copy(u):
        return pltpu.make_async_remote_copy(
            src_ref=made.at[u, pl.ds(BLOCK - EDGE, EDGE), :],
            dst_ref=edge.at[u],
            send_sem=edge_send.at[u],
            recv_sem=edge_recv.at[u],
            device_id={"pipe": section + 1, "ctx": mine + 1},
            device_id_type=MESH,
        )

    def state_copy(u):
        return pltpu.make_async_remote_copy(
            src_ref=state_out.at[u],
            dst_ref=state_in.at[u],
            send_sem=state_send.at[u],
            recv_sem=state_recv.at[u],
            device_id={"pipe": section, "ctx": mine + 1},
            device_id_type=MESH,
        )

    pl.semaphore_wait(barrier, count)

    @pl.when(has_right)
    def _():
        head_copy(bc_ref, bc_head, 0).start()
        head_copy(x_ref, x_head, 1).start()

    @pl.when(jnp.logical_not(has_left))
    def _():
        bc_head[...] = jnp.zeros_like(bc_head)
        x_head[...] = jnp.zeros_like(x_head)
        state_in[...] = jnp.zeros_like(state_in)

    @pl.when(jnp.logical_not(has_prev))
    def _():
        prev[...] = jnp.zeros_like(prev)

    @pl.when(jnp.logical_not(has_prev & has_left))
    def _():
        edge[...] = jnp.zeros_like(edge)

    rows = lax.broadcasted_iota(jnp.int32, (BLOCK, BLOCK), 0)
    cols = lax.broadcasted_iota(jnp.int32, (BLOCK, BLOCK), 1)
    lower = rows >= cols
    raw = jnp.concatenate([dt_ref[0, s] for s in range(SEQS)], axis=1)
    steps = jnp.maximum(raw, 0.0) + jnp.log1p(jnp.exp(-jnp.abs(raw)))
    rates = jnp.concatenate([rate_ref[...]] * SEQS, axis=1)
    cum = jnp.dot(
        lower.astype(f32), -steps * rates, precision=HIGHEST, preferred_element_type=f32
    )
    cum_t[...] = cum.T
    dt_t[...] = steps.T
    for u in range(UNITS):
        cum_cols[u] = cum[:, u * PER_GROUP : (u + 1) * PER_GROUP]
    grown = jnp.exp(cum)
    tail = jnp.exp(cum[BLOCK - 1 : BLOCK] - cum) * steps
    both = jnp.concatenate([grown, tail], axis=0)

    sk_rows = lax.broadcasted_iota(jnp.int32, (HEADS, HD), 0)
    sk_cols = lax.broadcasted_iota(jnp.int32, (HEADS, HD), 1)
    skips[...] = jnp.dot(
        jnp.broadcast_to(skip_ref[...], (8, HEADS)),
        (sk_rows == sk_cols // HEAD_DIM).astype(f32),
        precision=HIGHEST,
        preferred_element_type=f32,
    )

    @pl.when(has_left)
    def _():
        head_copy(bc_ref, bc_head, 0).wait_recv()
        head_copy(x_ref, x_head, 1).wait_recv()

    ex_rows = lax.broadcasted_iota(jnp.int32, (BLOCK, WIDTH), 0)
    ex_cols = lax.broadcasted_iota(jnp.int32, (BLOCK, WIDTH), 1)

    def prepare(i, carry):
        s, pair = i // (GROUPS // 2), i % (GROUPS // 2)
        acts = []
        for part in range(2):
            at = pl.multiple_of(part * GROUPS * STATE + pair * 2 * STATE, 2 * STATE)
            bbuf[part, pl.ds(0, EDGE), :] = bc_head[s, :, pl.ds(at, 2 * STATE)].astype(f32)
            bbuf[part, pl.ds(EDGE, BLOCK), :] = bc_ref[0, s, :, pl.ds(at, 2 * STATE)].astype(f32)
            weight = w_ref[0, :, pl.ds(pl.multiple_of(HD + at, 2 * STATE), 2 * STATE)]
            acts.append(conv(bbuf.at[part], weight).astype(bf16))
        b_t = acts[0].astype(f32).T.astype(bf16)
        for half in range(2):
            u = s * GROUPS + pair * 2 + half
            c_u = acts[1][:, half * STATE : (half + 1) * STATE]
            b_u = b_t[half * STATE : (half + 1) * STATE]
            c_rows[u] = c_u
            b_rows[u] = b_u
            scores = jnp.dot(c_u, b_u, preferred_element_type=f32)
            at = pl.multiple_of(u * PER_GROUP, PER_GROUP)
            c_t = cum_t[pl.ds(at, PER_GROUP), :]
            d_t = dt_t[pl.ds(at, PER_GROUP), :]
            c_c = cum_cols[u]
            for h in range(PER_GROUP):
                gap = c_c[:, h : h + 1] - c_t[h : h + 1, :]
                decay = jnp.exp(jnp.where(lower, gap, -1e30))
                weights[u, :, h * BLOCK : (h + 1) * BLOCK] = (
                    scores * decay * d_t[h : h + 1, :]
                ).astype(bf16)
            spread = (ex_rows == u * PER_GROUP + ex_cols // HEAD_DIM).astype(f32)
            wide = jnp.dot(both, spread, precision=HIGHEST, preferred_element_type=f32)
            ecum[u] = wide[:BLOCK]
            tails[u] = wide[BLOCK:]
        return carry

    lax.fori_loop(0, UNITS // 2, prepare, 0)

    lane_head = lax.broadcasted_iota(jnp.int32, (BLOCK, WIDTH), 1) // HEAD_DIM

    def unit(u, carry):
        s, g = u // GROUPS, u % GROUPS
        at = pl.multiple_of(g * WIDTH, WIDTH)
        lanes = pl.ds(at, WIDTH)

        @pl.when(has_prev)
        def _():
            prev_copy(u).wait_recv()

        @pl.when(has_prev & has_left)
        def _():
            edge_copy(u).wait_recv()

        cbuf[pl.ds(0, EDGE), :] = x_head[s, :, lanes].astype(f32) + edge[u].astype(f32)
        cbuf[pl.ds(EDGE, BLOCK), :] = x_ref[0, s, :, lanes].astype(f32) + prev[u].astype(f32)
        xs = conv(cbuf, w_ref[0, :, lanes]).astype(bf16)
        xs32 = xs.astype(f32)
        grow = ecum[u]
        local = jnp.dot(b_rows[u], (xs32 * tails[u]).astype(bf16), preferred_element_type=f32)

        @pl.when(has_left)
        def _():
            state_copy(u).wait_recv()

        incoming = state_in[u].astype(f32)
        state_out[u] = (grow[BLOCK - 1 : BLOCK] * incoming + local).astype(STATE_DT)

        @pl.when(has_right)
        def _():
            state_copy(u).start()

        zero = jnp.zeros_like(xs)
        diagonal = jnp.concatenate(
            [jnp.where(lane_head == h, xs, zero) for h in range(PER_GROUP)], axis=0
        )
        mixed = jnp.dot(weights[u], diagonal, preferred_element_type=f32)
        off = jnp.dot(c_rows[u], incoming.astype(bf16), preferred_element_type=f32)
        mixed = mixed + off * grow + skips[0:1, lanes] * xs32
        gated = mixed * silu(gate_ref[0, s, :, lanes].astype(f32))
        mean = jnp.sum(gated * gated, axis=1, keepdims=True) * (1.0 / WIDTH)
        result = (gated * lax.rsqrt(mean + norm_eps) * gain_ref[0:1, lanes]).astype(bf16)
        made[u] = result

        @pl.when(has_next)
        def _():
            prev_copy(u).start()

        @pl.when(has_next & has_right)
        def _():
            edge_copy(u).start()

        out_ref[0, s, :, lanes] = result
        return carry

    lax.fori_loop(0, UNITS, unit, 0)

    @pl.when(has_right)
    def _():
        head_copy(bc_ref, bc_head, 0).wait_send()
        head_copy(x_ref, x_head, 1).wait_send()

    def drain(u, carry):
        @pl.when(has_right)
        def _():
            state_copy(u).wait_send()

        @pl.when(has_next)
        def _():
            prev_copy(u).wait_send()

        @pl.when(has_next & has_right)
        def _():
            edge_copy(u).wait_send()

        return carry

    lax.fori_loop(0, UNITS, drain, 0)


def solution(mesh):
    sections, ranges = mesh.shape["pipe"], mesh.shape["ctx"]
    f32, bf16 = jnp.float32, jnp.bfloat16
    vmem = pl.BlockSpec(memory_space=pltpu.VMEM)
    dma = pltpu.SemaphoreType.DMA

    def on_device(x, gate, bc, dt, rate, weight, skip, gain):
        return pl.pallas_call(
            functools.partial(kernel, sections, ranges),
            out_shape=jax.ShapeDtypeStruct(x.shape, bf16),
            in_specs=[vmem] * 8,
            out_specs=vmem,
            scratch_shapes=[
                pltpu.VMEM((UNITS, BLOCK, PER_GROUP * BLOCK), bf16),
                pltpu.VMEM((UNITS, STATE, BLOCK), bf16),
                pltpu.VMEM((UNITS, BLOCK, STATE), bf16),
                pltpu.VMEM((UNITS, BLOCK, WIDTH), f32),
                pltpu.VMEM((UNITS, BLOCK, WIDTH), f32),
                pltpu.VMEM((UNITS, BLOCK, PER_GROUP), f32),
                pltpu.VMEM((BLOCK, BLOCK), f32),
                pltpu.VMEM((BLOCK, BLOCK), f32),
                pltpu.VMEM((8, HD), f32),
                pltpu.VMEM((EDGE + BLOCK, WIDTH), f32),
                pltpu.VMEM((2, EDGE + BLOCK, 2 * STATE), f32),
                pltpu.VMEM((SEQS, EDGE, HD), bf16),
                pltpu.VMEM((SEQS, EDGE, 2 * GROUPS * STATE), bf16),
                pltpu.VMEM((UNITS, BLOCK, WIDTH), bf16),
                pltpu.VMEM((UNITS, EDGE, WIDTH), bf16),
                pltpu.VMEM((UNITS, STATE, WIDTH), STATE_DT),
                pltpu.VMEM((UNITS, STATE, WIDTH), STATE_DT),
                pltpu.VMEM((UNITS, BLOCK, WIDTH), bf16),
                dma((2,)),
                dma((2,)),
                dma((UNITS,)),
                dma((UNITS,)),
                dma((UNITS,)),
                dma((UNITS,)),
                dma((UNITS,)),
                dma((UNITS,)),
            ],
            compiler_params=pltpu.CompilerParams(
                collective_id=0, has_side_effects=True, vmem_limit_bytes=48 * 1024 * 1024
            ),
            name="relay",
        )(x, gate, bc, dt, rate, weight, skip, gain)

    rows = P("pipe", None, "ctx", None)
    in_specs = (rows, rows, rows, rows, P("pipe", None), P("pipe", None, None), P("pipe", None), P("pipe", None))
    return jax.shard_map(on_device, mesh=mesh, in_specs=in_specs, out_specs=rows, check_vma=False)
```

time: 834 us -> 73.2 us (0.09); the launches traced: 821 us -> 72.9 us
  waiting for transfers between devices: 578 us -> 0 us
  other arithmetic: 83.7 us -> 0 us
  Pallas kernels: 0 us -> 67.4 us
  blocking collectives: 62.3 us -> 0 us
  local copies, waits for them, and re-layouts: 50.1 us -> 5.46 us
  matrix products: 18.1 us -> 0 us
  between operations: 13.1 us -> 0.07 us
  starting transfers between devices: 12.9 us -> 0 us
    all_gather x5 -> x0, waiting for transfers between devices: 552 us -> none  [carried_in(): everything = jax.tree.map(lambda part: lax.all_gather(part, axis), x)]
    pallas_call x0 -> x1, Pallas kernels: none -> 67.4 us  [on_device(): pl.pallas_call(functools.partial(kernel, sections, ranges), out_shape=jax...]
    all_gather x5 -> x0, blocking collectives: 62.3 us -> none  [carried_in(): everything = jax.tree.map(lambda part: lax.all_gather(part, axis), x)]
    select_n x45 -> x0, other arithmetic: 61.8 us -> none  [the longest x40 59.3 us: turn(): return jax.tree.map(lambda a, b: jnp.where(reached, a, b), new, before)]
    ppermute x10 -> x0, waiting for transfers between devices: 25.8 us -> none  [from_behind(): return lax.ppermute(block, axis, route)]
    convert_element_type x30 -> x0, other arithmetic: 18.8 us -> none  [the longest x5 7.35 us: block_terms(): weights = (scores * decays * dt_heads[:, :, None, :]).astype(jnp.bfloat16)]
    dot_general x20 -> x0, matrix products: 18.1 us -> none  [the longest x5 8.28 us: block_terms(): jnp.einsum('cqhn,cqhp->chpn', keyed_rows, inputs_x, preferred_element_typ...]
    ppermute x10 -> x0, starting transfers between devices: 12.9 us -> none  [from_behind(): return lax.ppermute(block, axis, route)]
  transfers between devices with their start and end apart: 15 -> 0, of which waited for: 15 -> 0; matrix products, arithmetic and copies ran while one was open for 5% -> 0% of each run, Pallas kernels for 0% -> 0%
where the time goes in v1:
time: 73.2 us; the launch traced here: 72.9 us
  Pallas kernels  67.4 us (92%)
  local copies, waits for them, and re-layouts  5.46 us (7%)
    pallas_call x1, Pallas kernels, on_device(): pl.pallas_call(functools.partial(kernel, sections, ranges), out_shape=jax...  67.4 us
    unnamed x16, local copies, waits for them, and re-layouts  5.46 us

profile of v1, /device:TPU:31, one launch (start us, length us, event | category | flops | bytes accessed | tf_op | source)
XLA Modules:
  0.0 72.9 jit_solution(12666537347942617738)
XLA Ops:
  0.0 0.0 copy-start.4
  0.0 0.0 copy-start.6
  0.0 0.0 copy-start.3
  0.0 0.0 copy-start.5
  0.0 1.0 %copy.9.dt_ref = f32[1,2,128,64]{3,2,1,0:T(8,128)S(1)} copy(f32[1,2,128,64]{2,3,1,0:T(8,128)} %param.11) | data formatting | bytes 131072 | tf_op args[3]
  1.0 0.0 copy-done.4
  1.0 0.0 copy-done.6
  1.0 0.0 copy-done.3
  1.0 0.0 copy-done.5
  1.1 0.0 copy-start
  1.1 1.2 %copy-done = bf16[1,2,128,2048]{3,2,1,0:T(8,128)(2,1)S(1)} copy-done((bf16[1,2,128,2048]{3,2,1,0:T(8,128)(2,1)S(1)}, bf16[1,2,128,2048]{3,2,1,0:T(8,128)(2,1)}, u32[]{:S(2)}) %copy-start) | copy-done | bytes 1048600
  2.3 0.0 copy-start.1
  2.3 1.2 %copy-done.1 = bf16[1,2,128,2048]{3,2,1,0:T(8,128)(2,1)S(1)} copy-done((bf16[1,2,128,2048]{3,2,1,0:T(8,128)(2,1)S(1)}, bf16[1,2,128,2048]{3,2,1,0:T(8,128)(2,1)}, u32[]{:S(2)}) %copy-start.1) | copy-done | bytes 1048600
  3.5 0.0 copy-start.2
  3.5 1.0 %copy-done.2 = bf16[1,2,128,1024]{3,2,1,0:T(8,128)(2,1)S(1)} copy-done((bf16[1,2,128,1024]{3,2,1,0:T(8,128)(2,1)S(1)}, bf16[1,2,128,1024]{3,2,1,0:T(8,128)(2,1)}, u32[]{:S(2)}) %copy-start.2) | copy-done | bytes 524312
  4.5 67.4 %relay.1 = bf16[1,2,128,2048]{3,2,1,0:T(8,128)(2,1)S(1)} custom-call(bf16[1,2,128,2048]{3,2,1,0:T(8,128)(2,1)S(1)} %copy-done, bf16[1,2,128,2048]{3,2,1,0:T(8,128)(2,1)S(1)} %copy-done.1, bf16[1,2,128,1024]{3,2,1,0:T(8,128)(2,1)S(1)} %copy-done.2, f32[1,2,128,64]{3,2,1,0:T(8,128)S(1)} %copy.9.dt_ref, f32[1,64]{1,0:T(1,128)S(1)} %copy-done.5, ...), custom_call_target="tpu_custom_call" | custom-call | tf_op jit(solution)/shard_map/relay/pallas_call | solution.py:329
  72.0 1.0 %copy.11 = bf16[1,2,128,2048]{3,2,1,0:T(8,128)(2,1)} copy(bf16[1,2,128,2048]{3,2,1,0:T(8,128)(2,1)S(1)} %relay.1) | data formatting | bytes 2097152
Async XLA Ops:
  0.0 1.0 %copy-start.4 = (f32[1,2048]{1,0:T(1,128)S(1)}, f32[1,2048]{1,0:T(1,128)}, u32[]{:S(2)}) copy-start(f32[1,2048]{1,0:T(1,128)} %gain_ref.1) | copy-start | bytes 24580
  0.0 1.0 %copy-start.6 = (f32[1,64]{1,0:T(1,128)S(1)}, f32[1,64]{1,0:T(1,128)}, u32[]{:S(2)}) copy-start(f32[1,64]{1,0:T(1,128)} %skip_ref.1) | copy-start | bytes 772
  0.0 1.0 %copy-start.3 = (f32[1,4,3072]{2,1,0:T(4,128)S(1)}, f32[1,4,3072]{2,1,0:T(4,128)}, u32[]{:S(2)}) copy-start(f32[1,4,3072]{2,1,0:T(4,128)} %w_ref.1) | copy-start | bytes 147460
  0.0 1.0 %copy-start.5 = (f32[1,64]{1,0:T(1,128)S(1)}, f32[1,64]{1,0:T(1,128)}, u32[]{:S(2)}) copy-start(f32[1,64]{1,0:T(1,128)} %rate_ref.1) | copy-start | bytes 772
  1.1 1.2 %copy-start = (bf16[1,2,128,2048]{3,2,1,0:T(8,128)(2,1)S(1)}, bf16[1,2,128,2048]{3,2,1,0:T(8,128)(2,1)}, u32[]{:S(2)}) copy-start(bf16[1,2,128,2048]{3,2,1,0:T(8,128)(2,1)} %x_ref.1) | copy-start | bytes 3145732
  2.3 1.2 %copy-start.1 = (bf16[1,2,128,2048]{3,2,1,0:T(8,128)(2,1)S(1)}, bf16[1,2,128,2048]{3,2,1,0:T(8,128)(2,1)}, u32[]{:S(2)}) copy-start(bf16[1,2,128,2048]{3,2,1,0:T(8,128)(2,1)} %gate_ref.1) | copy-start | bytes 3145732
  3.5 1.0 %copy-start.2 = (bf16[1,2,128,1024]{3,2,1,0:T(8,128)(2,1)S(1)}, bf16[1,2,128,1024]{3,2,1,0:T(8,128)(2,1)}, u32[]{:S(2)}) copy-start(bf16[1,2,128,1024]{3,2,1,0:T(8,128)(2,1)} %bc_ref.1) | copy-start | bytes 1572868

commit v2 on v1

--- a/solution.py
+++ b/solution.py
@@ -23,7 +23,7 @@
 norm_eps = 1e-05
 MESH = pl.DeviceIdType.MESH
 HIGHEST = lax.Precision.HIGHEST
-STATE_DT = jnp.float32
+STATE_DT = jnp.bfloat16
 
 
 def silu(v):
@@ -42,15 +42,19 @@
 def kernel(
     sections,
     ranges,
-    x_ref,
-    gate_ref,
-    bc_ref,
+    x_hbm,
+    gate_hbm,
+    bc_hbm,
     dt_ref,
     rate_ref,
     w_ref,
     skip_ref,
     gain_ref,
-    out_ref,
+    out_hbm,
+    x_ref,
+    gate_ref,
+    bc_ref,
+    fades,
     weights,
     b_rows,
     c_rows,
@@ -69,6 +73,8 @@
     state_in,
     state_out,
     made,
+    fetch_sem,
+    out_sem,
     head_send,
     head_recv,
     prev_send,
@@ -86,6 +92,10 @@
     has_right = mine < ranges - 1
     has_left = mine > 0
 
+    fetches = [
+        pltpu.make_async_copy(src, dst, fetch_sem.at[i])
+        for i, (src, dst) in enumerate(((bc_hbm, bc_ref), (x_hbm, x_ref), (gate_hbm, gate_ref)))
+    ]
     barrier = pltpu.get_barrier_semaphore()
     partners = (
         (has_next, 1, 0),
@@ -108,6 +118,12 @@
                 device_id_type=MESH,
             )
 
+    def out_copy(u):
+        lanes = pl.ds(pl.multiple_of((u % GROUPS) * WIDTH, WIDTH), WIDTH)
+        return pltpu.make_async_copy(
+            made.at[u], out_hbm.at[0, u // GROUPS, :, lanes], out_sem.at[u]
+        )
+
     def head_copy(src, dst, slot):
         return pltpu.make_async_remote_copy(
             src_ref=src.at[0, :, pl.ds(BLOCK - EDGE, EDGE), :],
@@ -148,6 +164,54 @@
             device_id_type=MESH,
         )
 
+    for fetch in fetches:
+        fetch.start()
+
+    rows = lax.broadcasted_iota(jnp.int32, (BLOCK, BLOCK), 0)
+    cols = lax.broadcasted_iota(jnp.int32, (BLOCK, BLOCK), 1)
+    lower = rows >= cols
+    raw = jnp.concatenate([dt_ref[0, s] for s in range(SEQS)], axis=0)
+    steps = jnp.maximum(raw, 0.0) + jnp.log1p(jnp.exp(-jnp.abs(raw)))
+    rates = jnp.concatenate([rate_ref[...]] * SEQS, axis=1)
+    rates = jnp.broadcast_to(rates, (BLOCK, SEQS * HEADS)).T
+    summed = jnp.dot(
+        -steps * rates,
+        (rows <= cols).astype(f32),
+        precision=HIGHEST,
+        preferred_element_type=f32,
+    )
+    cum_t[...] = summed
+    dt_t[...] = steps
+    cum = summed.T
+    for u in range(UNITS):
+        cum_cols[u] = cum[:, u * PER_GROUP : (u + 1) * PER_GROUP]
+    grown = jnp.exp(cum)
+    tail = jnp.exp(cum[BLOCK - 1 : BLOCK] - cum) * steps.T
+    both = jnp.concatenate([grown, tail], axis=0)
+    high = both.astype(bf16)
+    pair_of = jnp.concatenate([high, (both - high.astype(f32)).astype(bf16)], axis=1)
+    ex_rows = lax.broadcasted_iota(jnp.int32, (2 * BLOCK, WIDTH), 0) % BLOCK
+    ex_cols = lax.broadcasted_iota(jnp.int32, (2 * BLOCK, WIDTH), 1) // HEAD_DIM
+
+    def fade(u, carry):
+        at = pl.multiple_of(u * PER_GROUP, PER_GROUP)
+        c_t = cum_t[pl.ds(at, PER_GROUP), :]
+        d_t = dt_t[pl.ds(at, PER_GROUP), :]
+        c_c = cum_cols[u]
+        for h in range(PER_GROUP):
+            gap = c_c[:, h : h + 1] - c_t[h : h + 1, :]
+            decay = jnp.exp(jnp.where(lower, gap, -1e30))
+            fades[u, :, h * BLOCK : (h + 1) * BLOCK] = decay * d_t[h : h + 1, :]
+        spread = (ex_rows == u * PER_GROUP + ex_cols).astype(bf16)
+        wide = jnp.dot(pair_of, spread, preferred_element_type=f32)
+        ecum[u] = wide[:BLOCK]
+        tails[u] = wide[BLOCK:]
+        return carry
+
+    lax.fori_loop(0, UNITS // 2, fade, 0)
+
+    for fetch in fetches:
+        fetch.wait()
     pl.semaphore_wait(barrier, count)
 
     @pl.when(has_right)
@@ -169,22 +233,7 @@
     def _():
         edge[...] = jnp.zeros_like(edge)
 
-    rows = lax.broadcasted_iota(jnp.int32, (BLOCK, BLOCK), 0)
-    cols = lax.broadcasted_iota(jnp.int32, (BLOCK, BLOCK), 1)
-    lower = rows >= cols
-    raw = jnp.concatenate([dt_ref[0, s] for s in range(SEQS)], axis=1)
-    steps = jnp.maximum(raw, 0.0) + jnp.log1p(jnp.exp(-jnp.abs(raw)))
-    rates = jnp.concatenate([rate_ref[...]] * SEQS, axis=1)
-    cum = jnp.dot(
-        lower.astype(f32), -steps * rates, precision=HIGHEST, preferred_element_type=f32
-    )
-    cum_t[...] = cum.T
-    dt_t[...] = steps.T
-    for u in range(UNITS):
-        cum_cols[u] = cum[:, u * PER_GROUP : (u + 1) * PER_GROUP]
-    grown = jnp.exp(cum)
-    tail = jnp.exp(cum[BLOCK - 1 : BLOCK] - cum) * steps
-    both = jnp.concatenate([grown, tail], axis=0)
+    lax.fori_loop(UNITS // 2, UNITS, fade, 0)
 
     sk_rows = lax.broadcasted_iota(jnp.int32, (HEADS, HD), 0)
     sk_cols = lax.broadcasted_iota(jnp.int32, (HEADS, HD), 1)
@@ -199,9 +248,6 @@
     def _():
         head_copy(bc_ref, bc_head, 0).wait_recv()
         head_copy(x_ref, x_head, 1).wait_recv()
-
-    ex_rows = lax.broadcasted_iota(jnp.int32, (BLOCK, WIDTH), 0)
-    ex_cols = lax.broadcasted_iota(jnp.int32, (BLOCK, WIDTH), 1)
 
     def prepare(i, carry):
         s, pair = i // (GROUPS // 2), i % (GROUPS // 2)
@@ -220,20 +266,9 @@
             c_rows[u] = c_u
             b_rows[u] = b_u
             scores = jnp.dot(c_u, b_u, preferred_element_type=f32)
-            at = pl.multiple_of(u * PER_GROUP, PER_GROUP)
-            c_t = cum_t[pl.ds(at, PER_GROUP), :]
-            d_t = dt_t[pl.ds(at, PER_GROUP), :]
-            c_c = cum_cols[u]
             for h in range(PER_GROUP):
-                gap = c_c[:, h : h + 1] - c_t[h : h + 1, :]
-                decay = jnp.exp(jnp.where(lower, gap, -1e30))
-                weights[u, :, h * BLOCK : (h + 1) * BLOCK] = (
-                    scores * decay * d_t[h : h + 1, :]
-                ).astype(bf16)
-            spread = (ex_rows == u * PER_GROUP + ex_cols // HEAD_DIM).astype(f32)
-            wide = jnp.dot(both, spread, precision=HIGHEST, preferred_element_type=f32)
-            ecum[u] = wide[:BLOCK]
-            tails[u] = wide[BLOCK:]
+                lanes = slice(h * BLOCK, (h + 1) * BLOCK)
+                weights[u, :, lanes] = (scores * fades[u, :, lanes]).astype(bf16)
         return carry
 
     lax.fori_loop(0, UNITS // 2, prepare, 0)
@@ -291,7 +326,7 @@
         def _():
             edge_copy(u).start()
 
-        out_ref[0, s, :, lanes] = result
+        out_copy(u).start()
         return carry
 
     lax.fori_loop(0, UNITS, unit, 0)
@@ -302,6 +337,8 @@
         head_copy(x_ref, x_head, 1).wait_send()
 
     def drain(u, carry):
+        out_copy(u).wait()
+
         @pl.when(has_right)
         def _():
             state_copy(u).wait_send()
@@ -323,15 +360,20 @@
     sections, ranges = mesh.shape["pipe"], mesh.shape["ctx"]
     f32, bf16 = jnp.float32, jnp.bfloat16
     vmem = pl.BlockSpec(memory_space=pltpu.VMEM)
+    hbm = pl.BlockSpec(memory_space=pltpu.HBM)
     dma = pltpu.SemaphoreType.DMA
 
     def on_device(x, gate, bc, dt, rate, weight, skip, gain):
         return pl.pallas_call(
             functools.partial(kernel, sections, ranges),
             out_shape=jax.ShapeDtypeStruct(x.shape, bf16),
-            in_specs=[vmem] * 8,
-            out_specs=vmem,
+            in_specs=[hbm] * 3 + [vmem] * 5,
+            out_specs=hbm,
             scratch_shapes=[
+                pltpu.VMEM(x.shape, bf16),
+                pltpu.VMEM(gate.shape, bf16),
+                pltpu.VMEM(bc.shape, bf16),
+                pltpu.VMEM((UNITS, BLOCK, PER_GROUP * BLOCK), f32),
                 pltpu.VMEM((UNITS, BLOCK, PER_GROUP * BLOCK), bf16),
                 pltpu.VMEM((UNITS, STATE, BLOCK), bf16),
                 pltpu.VMEM((UNITS, BLOCK, STATE), bf16),
@@ -350,6 +392,8 @@
                 pltpu.VMEM((UNITS, STATE, WIDTH), STATE_DT),
                 pltpu.VMEM((UNITS, STATE, WIDTH), STATE_DT),
                 pltpu.VMEM((UNITS, BLOCK, WIDTH), bf16),
+                dma((3,)),
+                dma((UNITS,)),
                 dma((2,)),
                 dma((2,)),
                 dma((UNITS,)),
@@ -360,10 +404,10 @@
                 dma((UNITS,)),
             ],
             compiler_params=pltpu.CompilerParams(
-                collective_id=0, has_side_effects=True, vmem_limit_bytes=48 * 1024 * 1024
+                collective_id=0, has_side_effects=True, vmem_limit_bytes=60 * 1024 * 1024
             ),
             name="relay",
-        )(x, gate, bc, dt, rate, weight, skip, gain)
+        )(x, gate, bc, jnp.swapaxes(dt, 2, 3), rate, weight, skip, gain)
 
     rows = P("pipe", None, "ctx", None)
     in_specs = (rows, rows, rows, rows, P("pipe", None), P("pipe", None, None), P("pipe", None), P("pipe", None))

time: 73.2 us -> 53.9 us (0.74)
  Pallas kernels: 67.4 us -> 51.3 us
  local copies, waits for them, and re-layouts: 5.46 us -> 2.3 us
    pallas_call x1, Pallas kernels: 67.4 us -> 51.3 us  [on_device(): pl.pallas_call(functools.partial(kernel, sections, ranges), out_shape=jax...]
    unnamed x16 -> x1, local copies, waits for them, and re-layouts: 5.46 us -> 2.3 us
where the time goes in v2:
time: 53.9 us; the launch traced here: 53.7 us
  Pallas kernels  51.3 us (95%)
  local copies, waits for them, and re-layouts  2.3 us (4%)
    pallas_call x1, Pallas kernels, on_device(): pl.pallas_call(functools.partial(kernel, sections, ranges), out_shape=jax...  51.3 us
    unnamed x1, local copies, waits for them, and re-layouts  2.3 us

profile of v2, /device:TPU:31, one launch (start us, length us, event | category | flops | bytes accessed | tf_op | source)
XLA Modules:
  0.0 53.7 jit_solution(10903793315675203304)
XLA Ops:
  0.0 51.3 %relay.1 = bf16[1,2,128,2048]{3,2,1,0:T(8,128)(2,1)} custom-call(bf16[1,2,128,2048]{3,2,1,0:T(8,128)(2,1)} %x_hbm.1, bf16[1,2,128,2048]{3,2,1,0:T(8,128)(2,1)} %gate_hbm.1, bf16[1,2,128,1024]{3,2,1,0:T(8,128)(2,1)} %bc_hbm.1, f32[1,2,64,128]{3,2,1,0:T(8,128)} %bitcast.1, f32[1,64]{1,0:T(1,128)} %rate_ref.1, f32[1,4,3072]{2,1,0:T(4,128)} %w_ref.1, ...), custom_call_target="tpu_custom_call" | custom-call | tf_op jit(solution)/shard_map/relay/pallas_call | solution.py:367
  51.4 2.3 %copy.10 = bf16[1,2,128,2048]{3,2,1,0:T(8,128)(2,1)} copy(bf16[1,2,128,2048]{3,2,1,0:T(8,128)(2,1)} %relay.1) | data formatting | bytes 2097152

commit v3 on v2

--- a/solution.py
+++ b/solution.py
@@ -18,6 +18,8 @@
 HD = HEADS * HEAD_DIM
 UNITS = SEQS * GROUPS
 EDGE = 16
+KEPT = 4
+PAD = 8
 TAPS = 4
 
 norm_eps = 1e-05
@@ -32,7 +34,7 @@
 
 
 def conv(buf, weight):
-    first = EDGE - TAPS + 1
+    first = PAD - TAPS + 1
     total = weight[0:1] * buf[first : first + BLOCK]
     for tap in range(1, TAPS):
         total = total + weight[tap : tap + 1] * buf[first + tap : first + tap + BLOCK]
@@ -50,7 +52,7 @@
     w_ref,
     skip_ref,
     gain_ref,
-    out_hbm,
+    out_ref,
     x_ref,
     gate_ref,
     bc_ref,
@@ -66,15 +68,15 @@
     skips,
     cbuf,
     bbuf,
-    x_head,
-    bc_head,
+    head_out,
+    head_in,
+    heads,
     prev,
     edge,
     state_in,
     state_out,
     made,
     fetch_sem,
-    out_sem,
     head_send,
     head_recv,
     prev_send,
@@ -118,18 +120,12 @@
                 device_id_type=MESH,
             )
 
-    def out_copy(u):
-        lanes = pl.ds(pl.multiple_of((u % GROUPS) * WIDTH, WIDTH), WIDTH)
-        return pltpu.make_async_copy(
-            made.at[u], out_hbm.at[0, u // GROUPS, :, lanes], out_sem.at[u]
-        )
-
-    def head_copy(src, dst, slot):
+    def head_copy():
         return pltpu.make_async_remote_copy(
-            src_ref=src.at[0, :, pl.ds(BLOCK - EDGE, EDGE), :],
-            dst_ref=dst,
-            send_sem=head_send.at[slot],
-            recv_sem=head_recv.at[slot],
+            src_ref=head_out,
+            dst_ref=head_in,
+            send_sem=head_send,
+            recv_sem=head_recv,
             device_id={"pipe": section, "ctx": mine + 1},
             device_id_type=MESH,
         )
@@ -208,21 +204,25 @@
         tails[u] = wide[BLOCK:]
         return carry
 
-    lax.fori_loop(0, UNITS // 2, fade, 0)
-
-    for fetch in fetches:
-        fetch.wait()
+    lax.fori_loop(0, UNITS // 4, fade, 0)
+
+    fetches[0].wait()
+    fetches[1].wait()
+    for ref, at in ((x_ref, 0), (bc_ref, HD)):
+        width = ref.shape[3]
+        last = [
+            ref[0, s, BLOCK - EDGE :, :].astype(f32)[EDGE - KEPT :] for s in range(SEQS)
+        ]
+        head_out[:, at : at + width] = jnp.concatenate(last, axis=0).astype(bf16)
     pl.semaphore_wait(barrier, count)
 
     @pl.when(has_right)
     def _():
-        head_copy(bc_ref, bc_head, 0).start()
-        head_copy(x_ref, x_head, 1).start()
+        head_copy().start()
 
     @pl.when(jnp.logical_not(has_left))
     def _():
-        bc_head[...] = jnp.zeros_like(bc_head)
-        x_head[...] = jnp.zeros_like(x_head)
+        head_in[...] = jnp.zeros_like(head_in)
         state_in[...] = jnp.zeros_like(state_in)
 
     @pl.when(jnp.logical_not(has_prev))
@@ -233,7 +233,7 @@
     def _():
         edge[...] = jnp.zeros_like(edge)
 
-    lax.fori_loop(UNITS // 2, UNITS, fade, 0)
+    lax.fori_loop(UNITS // 4, UNITS, fade, 0)
 
     sk_rows = lax.broadcasted_iota(jnp.int32, (HEADS, HD), 0)
     sk_cols = lax.broadcasted_iota(jnp.int32, (HEADS, HD), 1)
@@ -246,18 +246,21 @@
 
     @pl.when(has_left)
     def _():
-        head_copy(bc_ref, bc_head, 0).wait_recv()
-        head_copy(x_ref, x_head, 1).wait_recv()
+        head_copy().wait_recv()
+
+    arrived = head_in[...].astype(f32)
+    for s in range(SEQS):
+        heads[s, PAD - KEPT :, :] = arrived[s * KEPT : (s + 1) * KEPT]
 
     def prepare(i, carry):
         s, pair = i // (GROUPS // 2), i % (GROUPS // 2)
         acts = []
         for part in range(2):
             at = pl.multiple_of(part * GROUPS * STATE + pair * 2 * STATE, 2 * STATE)
-            bbuf[part, pl.ds(0, EDGE), :] = bc_head[s, :, pl.ds(at, 2 * STATE)].astype(f32)
-            bbuf[part, pl.ds(EDGE, BLOCK), :] = bc_ref[0, s, :, pl.ds(at, 2 * STATE)].astype(f32)
-            weight = w_ref[0, :, pl.ds(pl.multiple_of(HD + at, 2 * STATE), 2 * STATE)]
-            acts.append(conv(bbuf.at[part], weight).astype(bf16))
+            wide = pl.ds(pl.multiple_of(HD + at, 2 * STATE), 2 * STATE)
+            bbuf[part, pl.ds(0, PAD), :] = heads[s, :, wide]
+            bbuf[part, pl.ds(PAD, BLOCK), :] = bc_ref[0, s, :, pl.ds(at, 2 * STATE)].astype(f32)
+            acts.append(conv(bbuf.at[part], w_ref[0, :, wide]).astype(bf16))
         b_t = acts[0].astype(f32).T.astype(bf16)
         for half in range(2):
             u = s * GROUPS + pair * 2 + half
@@ -273,6 +276,7 @@
 
     lax.fori_loop(0, UNITS // 2, prepare, 0)
 
+    fetches[2].wait()
     lane_head = lax.broadcasted_iota(jnp.int32, (BLOCK, WIDTH), 1) // HEAD_DIM
 
     def unit(u, carry):
@@ -288,8 +292,8 @@
         def _():
             edge_copy(u).wait_recv()
 
-        cbuf[pl.ds(0, EDGE), :] = x_head[s, :, lanes].astype(f32) + edge[u].astype(f32)
-        cbuf[pl.ds(EDGE, BLOCK), :] = x_ref[0, s, :, lanes].astype(f32) + prev[u].astype(f32)
+        cbuf[pl.ds(0, PAD), :] = heads[s, :, lanes] + edge[u].astype(f32)[EDGE - PAD :]
+        cbuf[pl.ds(PAD, BLOCK), :] = x_ref[0, s, :, lanes].astype(f32) + prev[u].astype(f32)
         xs = conv(cbuf, w_ref[0, :, lanes]).astype(bf16)
         xs32 = xs.astype(f32)
         grow = ecum[u]
@@ -326,19 +330,16 @@
         def _():
             edge_copy(u).start()
 
-        out_copy(u).start()
+        out_ref[0, s, :, lanes] = result
         return carry
 
     lax.fori_loop(0, UNITS, unit, 0)
 
     @pl.when(has_right)
     def _():
-        head_copy(bc_ref, bc_head, 0).wait_send()
-        head_copy(x_ref, x_head, 1).wait_send()
+        head_copy().wait_send()
 
     def drain(u, carry):
-        out_copy(u).wait()
-
         @pl.when(has_right)
         def _():
             state_copy(u).wait_send()
@@ -362,13 +363,14 @@
     vmem = pl.BlockSpec(memory_space=pltpu.VMEM)
     hbm = pl.BlockSpec(memory_space=pltpu.HBM)
     dma = pltpu.SemaphoreType.DMA
+    pin = functools.partial(pltpu.with_memory_space_constraint, memory_space=pltpu.HBM)
 
     def on_device(x, gate, bc, dt, rate, weight, skip, gain):
         return pl.pallas_call(
             functools.partial(kernel, sections, ranges),
             out_shape=jax.ShapeDtypeStruct(x.shape, bf16),
             in_specs=[hbm] * 3 + [vmem] * 5,
-            out_specs=hbm,
+            out_specs=vmem,
             scratch_shapes=[
                 pltpu.VMEM(x.shape, bf16),
                 pltpu.VMEM(gate.shape, bf16),
@@ -383,19 +385,19 @@
                 pltpu.VMEM((BLOCK, BLOCK), f32),
                 pltpu.VMEM((BLOCK, BLOCK), f32),
                 pltpu.VMEM((8, HD), f32),
-                pltpu.VMEM((EDGE + BLOCK, WIDTH), f32),
-                pltpu.VMEM((2, EDGE + BLOCK, 2 * STATE), f32),
-                pltpu.VMEM((SEQS, EDGE, HD), bf16),
-                pltpu.VMEM((SEQS, EDGE, 2 * GROUPS * STATE), bf16),
+                pltpu.VMEM((PAD + BLOCK, WIDTH), f32),
+                pltpu.VMEM((2, PAD + BLOCK, 2 * STATE), f32),
+                pltpu.VMEM((SEQS * KEPT, x.shape[3] + bc.shape[3]), bf16),
+                pltpu.VMEM((SEQS * KEPT, x.shape[3] + bc.shape[3]), bf16),
+                pltpu.VMEM((SEQS, PAD, x.shape[3] + bc.shape[3]), f32),
                 pltpu.VMEM((UNITS, BLOCK, WIDTH), bf16),
                 pltpu.VMEM((UNITS, EDGE, WIDTH), bf16),
                 pltpu.VMEM((UNITS, STATE, WIDTH), STATE_DT),
                 pltpu.VMEM((UNITS, STATE, WIDTH), STATE_DT),
                 pltpu.VMEM((UNITS, BLOCK, WIDTH), bf16),
                 dma((3,)),
-                dma((UNITS,)),
-                dma((2,)),
-                dma((2,)),
+                dma(()),
+                dma(()),
                 dma((UNITS,)),
                 dma((UNITS,)),
                 dma((UNITS,)),
@@ -404,10 +406,10 @@
                 dma((UNITS,)),
             ],
             compiler_params=pltpu.CompilerParams(
-                collective_id=0, has_side_effects=True, vmem_limit_bytes=60 * 1024 * 1024
+                collective_id=0, has_side_effects=True, vmem_limit_bytes=48 * 1024 * 1024
             ),
             name="relay",
-        )(x, gate, bc, jnp.swapaxes(dt, 2, 3), rate, weight, skip, gain)
+        )(pin(x), pin(gate), pin(bc), jnp.swapaxes(dt, 2, 3), rate, weight, skip, gain)
 
     rows = P("pipe", None, "ctx", None)
     in_specs = (rows, rows, rows, rows, P("pipe", None), P("pipe", None, None), P("pipe", None), P("pipe", None))

time: 53.9 us -> 54 us (level)
  local copies, waits for them, and re-layouts: 2.3 us -> 3.98 us
  Pallas kernels: 51.3 us -> 49.7 us
    unnamed x1 -> x11, local copies, waits for them, and re-layouts: 2.3 us -> 3.98 us
    pallas_call x1, Pallas kernels: 51.3 us -> 49.7 us  [on_device(): pl.pallas_call(functools.partial(kernel, sections, ranges), out_shape=jax...]
where the time goes in v3:
time: 54 us; the launch traced here: 53.7 us
  Pallas kernels  49.7 us (92%)
  local copies, waits for them, and re-layouts  3.98 us (7%)
    pallas_call x1, Pallas kernels, on_device(): pl.pallas_call(functools.partial(kernel, sections, ranges), out_shape=jax...  49.7 us
    unnamed x11, local copies, waits for them, and re-layouts  3.98 us

profile of v3, /device:TPU:31, one launch (start us, length us, event | category | flops | bytes accessed | tf_op | source)
XLA Modules:
  0.0 53.7 jit_solution(4214406173731039316)
XLA Ops:
  0.0 0.0 copy-start.4
  0.0 0.0 copy-start.3
  0.0 0.7 %copy-done.4 = f32[1,64]{1,0:T(1,128)S(1)} copy-done((f32[1,64]{1,0:T(1,128)S(1)}, f32[1,64]{1,0:T(1,128)}, u32[]{:S(2)}) %copy-start.4) | copy-done | bytes 280
  0.7 0.0 copy-done.3
  0.7 0.0 copy-start
  0.7 0.8 %copy-done = f32[1,2,128,64]{2,3,1,0:T(8,128)S(1)} copy-done((f32[1,2,128,64]{2,3,1,0:T(8,128)S(1)}, f32[1,2,128,64]{2,3,1,0:T(8,128)}, u32[]{:S(2)}) %copy-start) | copy-done | bytes 65560
  1.5 0.0 copy-start.1
  1.5 0.8 %copy-done.1 = f32[1,4,3072]{2,1,0:T(4,128)S(1)} copy-done((f32[1,4,3072]{2,1,0:T(4,128)S(1)}, f32[1,4,3072]{2,1,0:T(4,128)}, u32[]{:S(2)}) %copy-start.1) | copy-done | bytes 49176
  2.3 0.0 copy-start.2
  2.3 0.7 %copy-done.2 = f32[1,2048]{1,0:T(1,128)S(1)} copy-done((f32[1,2048]{1,0:T(1,128)S(1)}, f32[1,2048]{1,0:T(1,128)}, u32[]{:S(2)}) %copy-start.2) | copy-done | bytes 8216
  3.0 49.7 %relay.1 = bf16[1,2,128,2048]{3,2,1,0:T(8,128)(2,1)S(1)} custom-call(bf16[1,2,128,2048]{3,2,1,0:T(8,128)(2,1)} %x_hbm.1, bf16[1,2,128,2048]{3,2,1,0:T(8,128)(2,1)} %gate_hbm.1, bf16[1,2,128,1024]{3,2,1,0:T(8,128)(2,1)} %bc_hbm.1, f32[1,2,64,128]{3,2,1,0:T(8,128)S(1)} %bitcast.1, f32[1,64]{1,0:T(1,128)S(1)} %copy-done.3, f32[1,4,3072]{2,1,0:T(4,128)S(1)} %copy-done.1, ...), custom_call_target="tpu_custom_call" | custom-call | tf_op jit(solution)/shard_map/relay/pallas_call | solution.py:369
  52.7 1.0 %copy.10 = bf16[1,2,128,2048]{3,2,1,0:T(8,128)(2,1)} copy(bf16[1,2,128,2048]{3,2,1,0:T(8,128)(2,1)S(1)} %relay.1) | data formatting | bytes 2097152
Async XLA Ops:
  0.0 0.7 %copy-start.4 = (f32[1,64]{1,0:T(1,128)S(1)}, f32[1,64]{1,0:T(1,128)}, u32[]{:S(2)}) copy-start(f32[1,64]{1,0:T(1,128)} %skip_ref.1) | copy-start | bytes 772
  0.0 0.7 %copy-start.3 = (f32[1,64]{1,0:T(1,128)S(1)}, f32[1,64]{1,0:T(1,128)}, u32[]{:S(2)}) copy-start(f32[1,64]{1,0:T(1,128)} %rate_ref.1) | copy-start | bytes 772
  0.7 0.8 %copy-start = (f32[1,2,128,64]{2,3,1,0:T(8,128)S(1)}, f32[1,2,128,64]{2,3,1,0:T(8,128)}, u32[]{:S(2)}) copy-start(f32[1,2,128,64]{2,3,1,0:T(8,128)} %param.11) | copy-start | bytes 196612
  1.5 0.8 %copy-start.1 = (f32[1,4,3072]{2,1,0:T(4,128)S(1)}, f32[1,4,3072]{2,1,0:T(4,128)}, u32[]{:S(2)}) copy-start(f32[1,4,3072]{2,1,0:T(4,128)} %w_ref.1) | copy-start | bytes 147460
  2.3 0.7 %copy-start.2 = (f32[1,2048]{1,0:T(1,128)S(1)}, f32[1,2048]{1,0:T(1,128)}, u32[]{:S(2)}) copy-start(f32[1,2048]{1,0:T(1,128)} %gain_ref.1) | copy-start | bytes 24580

commit v4 on v3

--- a/solution.py
+++ b/solution.py
@@ -47,12 +47,17 @@
     x_hbm,
     gate_hbm,
     bc_hbm,
+    dt_hbm,
+    rate_hbm,
+    w_hbm,
+    skip_hbm,
+    gain_hbm,
+    out_ref,
     dt_ref,
     rate_ref,
     w_ref,
     skip_ref,
     gain_ref,
-    out_ref,
     x_ref,
     gate_ref,
     bc_ref,
@@ -96,7 +101,18 @@
 
     fetches = [
         pltpu.make_async_copy(src, dst, fetch_sem.at[i])
-        for i, (src, dst) in enumerate(((bc_hbm, bc_ref), (x_hbm, x_ref), (gate_hbm, gate_ref)))
+        for i, (src, dst) in enumerate(
+            (
+                (dt_hbm, dt_ref),
+                (rate_hbm, rate_ref),
+                (bc_hbm, bc_ref),
+                (x_hbm, x_ref),
+                (w_hbm, w_ref),
+                (skip_hbm, skip_ref),
+                (gain_hbm, gain_ref),
+                (gate_hbm, gate_ref),
+            )
+        )
     ]
     barrier = pltpu.get_barrier_semaphore()
     partners = (
@@ -166,6 +182,8 @@
     rows = lax.broadcasted_iota(jnp.int32, (BLOCK, BLOCK), 0)
     cols = lax.broadcasted_iota(jnp.int32, (BLOCK, BLOCK), 1)
     lower = rows >= cols
+    fetches[0].wait()
+    fetches[1].wait()
     raw = jnp.concatenate([dt_ref[0, s] for s in range(SEQS)], axis=0)
     steps = jnp.maximum(raw, 0.0) + jnp.log1p(jnp.exp(-jnp.abs(raw)))
     rates = jnp.concatenate([rate_ref[...]] * SEQS, axis=1)
@@ -204,10 +222,10 @@
         tails[u] = wide[BLOCK:]
         return carry
 
-    lax.fori_loop(0, UNITS // 4, fade, 0)
-
-    fetches[0].wait()
-    fetches[1].wait()
+    lax.fori_loop(0, UNITS // 2, fade, 0)
+
+    fetches[2].wait()
+    fetches[3].wait()
     for ref, at in ((x_ref, 0), (bc_ref, HD)):
         width = ref.shape[3]
         last = [
@@ -233,8 +251,10 @@
     def _():
         edge[...] = jnp.zeros_like(edge)
 
-    lax.fori_loop(UNITS // 4, UNITS, fade, 0)
-
+    lax.fori_loop(UNITS // 2, UNITS, fade, 0)
+
+    for fetch in fetches[4:7]:
+        fetch.wait()
     sk_rows = lax.broadcasted_iota(jnp.int32, (HEADS, HD), 0)
     sk_cols = lax.broadcasted_iota(jnp.int32, (HEADS, HD), 1)
     skips[...] = jnp.dot(
@@ -276,7 +296,7 @@
 
     lax.fori_loop(0, UNITS // 2, prepare, 0)
 
-    fetches[2].wait()
+    fetches[7].wait()
     lane_head = lax.broadcasted_iota(jnp.int32, (BLOCK, WIDTH), 1) // HEAD_DIM
 
     def unit(u, carry):
@@ -369,9 +389,14 @@
         return pl.pallas_call(
             functools.partial(kernel, sections, ranges),
             out_shape=jax.ShapeDtypeStruct(x.shape, bf16),
-            in_specs=[hbm] * 3 + [vmem] * 5,
+            in_specs=[hbm] * 8,
             out_specs=vmem,
             scratch_shapes=[
+                pltpu.VMEM((1, SEQS, HEADS, BLOCK), f32),
+                pltpu.VMEM(rate.shape, f32),
+                pltpu.VMEM(weight.shape, f32),
+                pltpu.VMEM(skip.shape, f32),
+                pltpu.VMEM(gain.shape, f32),
                 pltpu.VMEM(x.shape, bf16),
                 pltpu.VMEM(gate.shape, bf16),
                 pltpu.VMEM(bc.shape, bf16),
@@ -395,7 +420,7 @@
                 pltpu.VMEM((UNITS, STATE, WIDTH), STATE_DT),
                 pltpu.VMEM((UNITS, STATE, WIDTH), STATE_DT),
                 pltpu.VMEM((UNITS, BLOCK, WIDTH), bf16),
-                dma((3,)),
+                dma((8,)),
                 dma(()),
                 dma(()),
                 dma((UNITS,)),
@@ -409,7 +434,7 @@
                 collective_id=0, has_side_effects=True, vmem_limit_bytes=48 * 1024 * 1024
             ),
             name="relay",
-        )(pin(x), pin(gate), pin(bc), jnp.swapaxes(dt, 2, 3), rate, weight, skip, gain)
+        )(*map(pin, (x, gate, bc, jnp.swapaxes(dt, 2, 3), rate, weight, skip, gain)))
 
     rows = P("pipe", None, "ctx", None)
     in_specs = (rows, rows, rows, rows, P("pipe", None), P("pipe", None, None), P("pipe", None), P("pipe", None))

time: 54 us -> 50.5 us (0.935)
  local copies, waits for them, and re-layouts: 3.98 us -> 0.97 us
    unnamed x11 -> x1, local copies, waits for them, and re-layouts: 3.98 us -> 0.97 us
where the time goes in v4:
time: 50.5 us; the launch traced here: 50.4 us
  Pallas kernels  49.4 us (98%)
  local copies, waits for them, and re-layouts  0.97 us (2%)
    pallas_call x1, Pallas kernels, on_device(): pl.pallas_call(functools.partial(kernel, sections, ranges), out_shape=jax...  49.4 us

profile of v4, /device:TPU:31, one launch (start us, length us, event | category | flops | bytes accessed | tf_op | source)
XLA Modules:
  0.0 50.4 jit_solution(12886912179054973366)
XLA Ops:
  0.0 49.4 %relay.1 = bf16[1,2,128,2048]{3,2,1,0:T(8,128)(2,1)S(1)} custom-call(bf16[1,2,128,2048]{3,2,1,0:T(8,128)(2,1)} %x_hbm.1, bf16[1,2,128,2048]{3,2,1,0:T(8,128)(2,1)} %gate_hbm.1, bf16[1,2,128,1024]{3,2,1,0:T(8,128)(2,1)} %bc_hbm.1, f32[1,2,64,128]{3,2,1,0:T(8,128)} %bitcast.1, f32[1,64]{1,0:T(1,128)} %rate_hbm.1, f32[1,4,3072]{2,1,0:T(4,128)} %w_hbm.1, ...), custom_call_target="tpu_custom_call" | custom-call | tf_op jit(solution)/shard_map/relay/pallas_call | solution.py:389
  49.4 1.0 %copy.10 = bf16[1,2,128,2048]{3,2,1,0:T(8,128)(2,1)} copy(bf16[1,2,128,2048]{3,2,1,0:T(8,128)(2,1)S(1)} %relay.1) | data formatting | bytes 2097152
